TPU v7x, 128 devices: a whole 4x4x4 slice. The times are simulated.
128 devices in a mesh: row: 8 (over y_lo, z), col: 2 (over y_hi), tensor: 8 (over x, core).
Axes of the slice: x: 4, y: 4 (y_hi: 2, y_lo: 2; y = y_hi * 2 + y_lo), z: 4, core: 2. Of those that a mesh axis runs over, the one named last changes fastest.
Arguments:
- tokens: bfloat16 [10240, 3072], P(('row', 'col', 'tensor')), may hold values from -6 to 6
- w_query: bfloat16 [3072, 3072], P(None, 'tensor'), may hold values from -0.109375 to 0.109375
- w_key: bfloat16 [3072, 3072], P(None, 'tensor'), may hold values from -0.109375 to 0.109375
- w_value: bfloat16 [3072, 3072], P(None, 'tensor'), may hold values from -0.109375 to 0.109375
- w_out: bfloat16 [3072, 3072], P('tensor'), may hold values from -0.109375 to 0.109375
- w_mod: bfloat16 [512, 18432], P(None, ('row', 'col', 'tensor')), may hold values from -2 to 2
- gain_query: float32 [64], replicated, may hold values from 0.5 to 2.5
- gain_key: float32 [64], replicated, may hold values from 0.5 to 2.5
- timesteps: int32 [2], replicated, may hold values from 0 to 999
- video_lengths: int32 [2], replicated, may hold values from 1 to 6117, 9788 in all
- piece_table: int32 [16], replicated, may hold values from 0 to 15, each once
Outputs:
- update: bfloat16 [10240, 3072], P(('row', 'col', 'tensor'))
Inputs may be any that keep to these rules, and one draw needn't show every extreme that they name: `video_lengths`: the two lengths sum to 9788; the larger one is at most 6117, and which sample has it varies. `piece_table`: each tile index 0 .. 15 appears once.
All inputs are finite; a program needn't handle non-finite values.
Results may differ from a plain program's by a relative error of at most 0.02.
Values may be sent and summed in bfloat16 or wider, within the bound.
No kernel may reach another device: no remote copies, remote signals or barrier semaphores. Data moves between devices by JAX's collectives and lax.ppermute only.
A program may use at most 192 MiB of HBM per device.

v0:
```python
import math
import jax
import jax.numpy as jnp
from jax import lax
from jax.sharding import PartitionSpec as P

HD = 64
TE = 512
TEXT = 226
HP = 30
WP = 45
CAP = 640


def slot_info(slot_ids, piece_table, video_lengths):
    tile_idx = slot_ids // CAP
    tile_total = piece_table.shape[0]
    placed = jnp.sum(
        jnp.where(
            tile_idx[:, None] == jnp.arange(tile_total, dtype=jnp.int32)[None, :],
            piece_table[None, :],
            0,
        ),
        axis=1,
    )
    token_id = placed * CAP + slot_ids % CAP
    boundary = TEXT + video_lengths[0]
    item_of = (token_id >= boundary).astype(jnp.int32)
    inner_idx = token_id - item_of * boundary
    is_text = inner_idx < TEXT
    video_idx = jnp.maximum(inner_idx - TEXT, 0)
    frame_idx = video_idx // (HP * WP)
    height_idx = video_idx // WP % HP
    width_idx = video_idx % WP
    return (item_of, is_text, frame_idx, height_idx, width_idx)


def time_features(timesteps):
    half_dim = TE // 2
    freqs = jnp.exp(-math.log(10000.0) * jnp.arange(half_dim, dtype=jnp.float32) / half_dim)
    angles = timesteps.astype(jnp.float32)[:, None] * freqs[None, :]
    return jnp.concatenate([jnp.cos(angles), jnp.sin(angles)], axis=1)


def rope_angles(frame_idx, height_idx, width_idx):
    time_dims = HD // 4
    space_dims = 3 * HD // 8
    freq_time = 10000.0 ** (-jnp.arange(0, time_dims, 2, dtype=jnp.float32) / time_dims)
    freq_space = 10000.0 ** (-jnp.arange(0, space_dims, 2, dtype=jnp.float32) / space_dims)
    return jnp.concatenate(
        [
            frame_idx.astype(jnp.float32)[:, None] * freq_time[None, :],
            height_idx.astype(jnp.float32)[:, None] * freq_space[None, :],
            width_idx.astype(jnp.float32)[:, None] * freq_space[None, :],
        ],
        axis=1,
    )


def head_prepare(projection, gain, angles, is_text):
    row_count = projection.shape[0]
    heads_here = projection.shape[1] // HD
    per_head = projection.reshape(row_count, heads_here, HD)
    center = per_head - jnp.mean(per_head, axis=2, keepdims=True)
    variance = jnp.mean(center * center, axis=2, keepdims=True)
    normed = center * lax.rsqrt(variance + 1e-06) * gain
    cosine = jnp.where(is_text[:, None], 1.0, jnp.cos(angles))[:, None, :]
    sine = jnp.where(is_text[:, None], 0.0, jnp.sin(angles))[:, None, :]
    paired = normed.reshape(row_count, heads_here, HD // 2, 2)
    even_part = paired[..., 0]
    odd_part = paired[..., 1]
    rotated = jnp.stack(
        [even_part * cosine - odd_part * sine, even_part * sine + odd_part * cosine], axis=-1
    )
    return rotated.reshape(row_count, heads_here * HD).astype(jnp.bfloat16)


def select_modulation(modulation, item_of, is_text, model_width):
    chosen = []
    for part_idx in range(3):
        video_cols = modulation[:, part_idx * model_width : (part_idx + 1) * model_width]
        text_cols = modulation[:, (part_idx + 3) * model_width : (part_idx + 4) * model_width]
        video_pick = jnp.where(
            item_of[:, None] == 1, video_cols[1][None, :], video_cols[0][None, :]
        )
        text_pick = jnp.where(item_of[:, None] == 1, text_cols[1][None, :], text_cols[0][None, :])
        chosen.append(jnp.where(is_text[:, None], text_pick, video_pick))
    return (chosen[0], chosen[1], chosen[2])


def modulate(tokens, shift, scale):
    values = tokens.astype(jnp.float32)
    center = values - jnp.mean(values, axis=1, keepdims=True)
    variance = jnp.mean(center * center, axis=1, keepdims=True)
    normed = center * lax.rsqrt(variance + 1e-05)
    return (normed * (1.0 + scale) + shift).astype(jnp.bfloat16)


def block_terms(query, key_part, value_part, same_item, heads_here):
    query_rows = query.shape[0]
    key_count = key_part.shape[0]
    query_heads = query.reshape(query_rows, heads_here, HD)
    key_heads = key_part.reshape(key_count, heads_here, HD)
    value_heads = value_part.reshape(key_count, heads_here, HD)
    scores = jnp.einsum(
        "qhd,khd->hqk", query_heads, key_heads, preferred_element_type=jnp.float32
    ) / math.sqrt(HD)
    weights = (jnp.exp(scores) * same_item[None, :, :]).astype(jnp.bfloat16)
    numer_add = jnp.einsum("hqk,khd->qhd", weights, value_heads, preferred_element_type=jnp.float32)
    denom_add = jnp.sum(weights.astype(jnp.float32), axis=2).T
    return (numer_add.reshape(query_rows, heads_here * HD), denom_add)


def local(
    tokens,
    w_query,
    w_key,
    w_value,
    w_out,
    w_mod,
    gain_query,
    gain_key,
    timesteps,
    video_lengths,
    piece_table,
):
    model_width = tokens.shape[1]
    act = jax.nn.silu(time_features(timesteps)).astype(jnp.bfloat16)
    partial_mod = jnp.dot(act, w_mod, preferred_element_type=jnp.float32)
    modulation = lax.all_gather(partial_mod, ("row", "col", "tensor"), axis=1, tiled=True)
    col_count = lax.axis_size("col")
    tile_here = lax.axis_index("row") * col_count + lax.axis_index("col")
    own_rows = tokens.shape[0]
    own_slots = (
        tile_here * CAP
        + lax.axis_index("tensor") * own_rows
        + jnp.arange(own_rows, dtype=jnp.int32)
    )
    own_item, own_text, own_frame, own_height, own_width = slot_info(
        own_slots, piece_table, video_lengths
    )
    shift, scale, gate = select_modulation(modulation, own_item, own_text, model_width)
    modded = modulate(tokens, shift, scale)
    pieces = lax.all_gather(modded, "tensor", axis=0, tiled=True)
    projected = jnp.concatenate(
        [
            jnp.dot(pieces, w_query, preferred_element_type=jnp.float32),
            jnp.dot(pieces, w_key, preferred_element_type=jnp.float32),
            jnp.dot(pieces, w_value, preferred_element_type=jnp.float32),
        ],
        axis=1,
    )
    local_width = w_query.shape[1]
    heads_here = local_width // HD
    tile_slots = tile_here * CAP + jnp.arange(CAP, dtype=jnp.int32)
    tile_item, tile_text, tile_frame, tile_height, tile_width = slot_info(
        tile_slots, piece_table, video_lengths
    )
    angles = rope_angles(tile_frame, tile_height, tile_width)
    query = head_prepare(projected[:, :local_width], gain_query, angles, tile_text)
    key_rows = head_prepare(
        projected[:, local_width : 2 * local_width], gain_key, angles, tile_text
    )
    value_rows = projected[:, 2 * local_width :].astype(jnp.bfloat16)
    key_block = lax.all_gather(key_rows, ("row", "col"), axis=0, tiled=True)
    value_block = lax.all_gather(value_rows, ("row", "col"), axis=0, tiled=True)
    numerator = jnp.zeros((CAP, local_width), jnp.float32)
    denominator = jnp.zeros((CAP, heads_here), jnp.float32)
    key_total = key_block.shape[0]
    key_slots = jnp.arange(key_total, dtype=jnp.int32)
    key_item, key_text, key_frame, key_height, key_width = slot_info(
        key_slots, piece_table, video_lengths
    )
    for offset in range(0, key_total, 512):
        stop = min(offset + 512, key_total)
        same_bool = tile_item[:, None] == key_item[None, offset:stop]
        same_item = same_bool.astype(jnp.float32)
        key_part = key_block[offset:stop]
        value_part = value_block[offset:stop]
        numer_add, denom_add = block_terms(query, key_part, value_part, same_item, heads_here)
        numerator = numerator + numer_add
        denominator = denominator + denom_add
    numerator, denominator = (numerator, denominator)
    attended = (numerator / jnp.repeat(denominator, HD, axis=1)).astype(jnp.bfloat16)
    projection = lax.psum_scatter(
        jnp.dot(attended, w_out, preferred_element_type=jnp.float32).astype(jnp.bfloat16),
        "tensor",
        scatter_dimension=0,
        tiled=True,
    ).astype(jnp.float32)
    return (gate * projection).astype(jnp.bfloat16)


def solution(mesh):
    placed = (
        P(("row", "col", "tensor"), None),
        P(None, "tensor"),
        P(None, "tensor"),
        P(None, "tensor"),
        P("tensor", None),
        P(None, ("row", "col", "tensor")),
        P(),
        P(),
        P(),
        P(),
        P(),
    )
    return jax.shard_map(
        local,
        mesh=mesh,
        in_specs=placed,
        out_specs=P(("row", "col", "tensor"), None),
        check_vma=False,
    )
```

profile of v0, /device:TPU:0, one launch (start us, length us, event | category | flops | bytes accessed | tf_op | source)
XLA Modules:
  0.0 762.9 jit_solution(14983908528028397755)
XLA Ops:
  12.6 179.5 %all-gather = f32[128,144,2]{1,2,0:T(2,128)S(1)} all-gather(f32[1,144,2]{1,2,0:T(2,128)S(1)} %convolution_bitcast_fusion.1), channel_id=1, replica_groups=mesh['row'=8,'col'=2,'tensor'=8] {'row','col','tensor'}, dimensions={0}, use_global_device_ids=true | all-gather | bytes 148608 | tf_op jit(solution)/shard_map/all_gather | solution.py:130
  195.5 24.6 %all-gather.5.cloned.1.call-done = bf16[640,3072]{1,0:T(8,128)(2,1)} async-done(((bf16[80,3072]{1,0:T(8,128)(2,1)}), bf16[640,3072]{1,0:T(8,128)(2,1)}) %all-gather.5.cloned.1.call-update) | async-done | bytes 3932176 | tf_op jit(solution)/shard_map/all_gather | solution.py:144
  220.2 5.8 convolution_convert_fusion.1
  228.5 4.9 fusion.47
  234.9 5.9 fusion.48
  249.0 3.3 subtract_convert_fusion
  256.6 8.8 %compare_convert_fusion.3 = (f32[640,512]{0,1:T(8,128)}, f32[640,512]{0,1:T(8,128)}, f32[640,512]{0,1:T(8,128)}, f32[640,512]{0,1:T(8,128)}, f32[640,512]{0,1:T(...) fusion(s32[640]{0:T(1024)S(1)} %get-tuple-element.105, ...), kind=kLoop, calls=%fused_computation.62 | loop fusion | flops 11796480 | bytes 23632384 | tf_op jit(solution)/shard_map/convert_element_type | solution.py:177
  267.5 161.6 %all-gather.7.cloned.1.call-done = bf16[10240,384]{1,0:T(8,128)(2,1)} async-done(((bf16[640,384]{1,0:T(8,128)(2,1)}), bf16[10240,384]{1,0:T(8,128)(2,1)}) %all-gather.7.cloned.1.call-update) | async-done | bytes 7864336 | tf_op jit(solution)/shard_map/all_gather | solution.py:166
  429.1 6.1 fusion.44
  469.6 152.2 %all-gather.9.cloned.1.call-done = bf16[10240,384]{0,1:T(8,128)(2,1)} async-done(((bf16[640,384]{0,1:T(8,128)(2,1)}), bf16[10240,384]{0,1:T(8,128)(2,1)}) %all-gather.9.cloned.1.call-update) | async-done | bytes 7864336 | tf_op jit(solution)/shard_map/all_gather | solution.py:165
  622.8 3.5 convert_reduce_fusion.19
  646.7 4.0 convert_reduce_fusion.12
  650.7 3.8 convert_reduce_fusion.11
  654.5 3.8 convert_reduce_fusion.10
  658.3 3.8 convert_reduce_fusion.9
  662.1 3.7 convert_reduce_fusion.8
  665.8 3.8 convert_reduce_fusion.7
  669.6 3.9 convert_reduce_fusion.6
  673.5 4.2 convert_reduce_fusion.5
  677.7 3.7 convert_reduce_fusion.4
  681.5 3.8 convert_reduce_fusion.2
  688.3 3.7 convert_reduce_fusion.1
  716.4 4.1 convolution_convert_fusion
  720.6 33.5 %reduce-scatter.2.cloned.1.call-done = bf16[80,3072]{1,0:T(8,128)(2,1)} async-done(((bf16[640,3072]{1,0:T(8,128)(2,1)}), bf16[80,3072]{1,0:T(8,128)(2,1)}) %reduce-scatter.2.cloned.1.call-update) | async-done | bytes 491536 | tf_op jit(solution)/shard_map/reduce_scatter | solution.py:185
  (252 shorter events, 111.8 us)
Async XLA Ops:
  6.5 709.9 %copy-start = (bf16[384,3072]{1,0:T(8,128)(2,1)S(1)}, bf16[384,3072]{1,0:T(8,128)(2,1)}, u32[]{:S(2)}) copy-start(bf16[384,3072]{1,0:T(8,128)(2,1)} %param.15) | copy-start | bytes 7077892
  6.5 213.6 %all-gather.5.cloned.1.call-start = ((), (), s32[]{:S(2)}) async-start(), calls=%async_computation.1 | async-start | bytes 4423680 | tf_op jit(solution)/shard_map/all_gather | solution.py:144
  11.4 214.6 %copy-start.62 = (pred[80]{0:T(512)(128)(4,1)}, pred[80]{0:T(512)(128)(4,1)S(1)}, u32[]{:S(2)}) copy-start(pred[80]{0:T(512)(128)(4,1)S(1)} %fusion.38) | copy-start | bytes 244
  195.4 30.9 %copy-start.66 = (f32[64]{0:T(128)S(1)}, f32[64]{0:T(128)}, u32[]{:S(2)}) copy-start(f32[64]{0:T(128)} %param.17) | copy-start | bytes 772
  195.4 31.6 %copy-start.67 = (f32[64]{0:T(128)S(1)}, f32[64]{0:T(128)}, u32[]{:S(2)}) copy-start(f32[64]{0:T(128)} %param.18) | copy-start | bytes 772
  195.5 32.4 %copy-start.64 = (s32[16]{0:T(128)S(1)}, s32[16]{0:T(128)}, u32[]{:S(2)}) copy-start(s32[16]{0:T(128)} %param.21) | copy-start | bytes 196
  195.5 233.7 %all-gather.7.cloned.1.call-start = ((), (), s32[]{:S(2)}) async-start(), calls=%async_computation.2 | async-start | bytes 8355840 | tf_op jit(solution)/shard_map/all_gather | solution.py:166
  226.0 395.8 %all-gather.9.cloned.1.call-start = ((), (), s32[]{:S(2)}) async-start(), calls=%async_computation.3 | async-start | bytes 8355840 | tf_op jit(solution)/shard_map/all_gather | solution.py:165
  249.0 5.5 copy-start.65
  254.4 499.6 %reduce-scatter.2.cloned.1.call-start = ((), (), s32[]{:S(2)}) async-start(), calls=%async_computation.4 | async-start | bytes 4423680 | tf_op jit(solution)/shard_map/reduce_scatter | solution.py:185
  256.6 8.8 %copy-start.10 = (bf16[640,6,32,1]{0,3,2,1:T(2,128)(2,1)S(1)}, bf16[640,6,32,1]{0,3,2,1:T(2,128)(2,1)}, u32[]{:S(2)}) copy-start(bf16[640,6,32,1]{0,3,2,1:T(2,128)(2,1)} %get-tuple-element.50) | copy-start | bytes 737284
  429.1 7.3 slice-start
  622.8 4.3 slice-start.1
  622.8 4.3 slice-start.2
  646.7 4.0 copy-start.38
  646.7 4.0 copy-start.55
  669.6 3.9 copy-start.32
  669.6 3.9 copy-start.49
  673.5 4.2 copy-start.31
  720.5 33.5 %copy-start.58 = (f32[1,3072]{1,0:T(1,128)S(1)}, f32[1,3072]{1,0:T(1,128)}, u32[]{:S(2)}) copy-start(f32[1,3072]{1,0:T(1,128)} %get-tuple-element.51) | copy-start | bytes 36868
  720.6 33.5 %copy-start.59 = (f32[1,3072]{1,0:T(1,128)S(1)}, f32[1,3072]{1,0:T(1,128)}, u32[]{:S(2)}) copy-start(f32[1,3072]{1,0:T(1,128)} %get-tuple-element.60) | copy-start | bytes 36868
  720.6 33.5 %copy-start.60 = (f32[1,3072]{1,0:T(1,128)S(1)}, f32[1,3072]{1,0:T(1,128)}, u32[]{:S(2)}) copy-start(f32[1,3072]{1,0:T(1,128)} %get-tuple-element.61) | copy-start | bytes 36868
  720.6 33.5 %copy-start.61 = (f32[1,3072]{1,0:T(1,128)S(1)}, f32[1,3072]{1,0:T(1,128)}, u32[]{:S(2)}) copy-start(f32[1,3072]{1,0:T(1,128)} %get-tuple-element.62) | copy-start | bytes 36868
  720.6 33.5 %copy-start.63 = (pred[80]{0:T(512)(128)(4,1)S(1)}, pred[80]{0:T(512)(128)(4,1)}, u32[]{:S(2)}) copy-start(pred[80]{0:T(512)(128)(4,1)} %copy-done.62) | copy-start | bytes 244
  (51 other events, 130.4 us)
Sparse Core Ops, SparseCore 0:
  195.6 24.5 all-gather.4
  226.1 202.9 all-gather.6
  430.8 190.9 all-gather.8
  720.7 33.2 reduce-scatter.1
where the time goes:
time: 768 us; the launch traced here: 763 us
  waiting for transfers between devices  372 us (48%)
  blocking collectives  180 us (23%)
  matrix products  104 us (14%)
  local copies, waits for them, and re-layouts  60.7 us (8%)
  other arithmetic  31.5 us (4%)
  between operations  15 us (2%)
    all_gather x1, blocking collectives, local(): lax.all_gather(partial_mod, ('row', 'col', 'tensor'), axis=1, tiled=True)  180 us
    all_gather x1, waiting for transfers between devices, local(): value_block = lax.all_gather(value_rows, ('row', 'col'), axis=0, tiled=True)  162 us
    all_gather x1, waiting for transfers between devices, local(): key_block = lax.all_gather(key_rows, ('row', 'col'), axis=0, tiled=True)  152 us
    dot_general x20, matrix products, block_terms(): jnp.einsum('qhd,khd->hqk', query_heads, key_heads, preferred_element_type...  61 us
    slice x23, local copies, waits for them, and re-layouts, local(): value_part = value_block[offset:stop]  40.4 us
    reduce_scatter x1, waiting for transfers between devices, local(): lax.psum_scatter(jnp.dot(attended, w_out, preferred_element_type=jnp.floa...  33.5 us
    all_gather x1, waiting for transfers between devices, local(): pieces = lax.all_gather(modded, 'tensor', axis=0, tiled=True)  24.6 us
    dot_general x20, matrix products, block_terms(): jnp.einsum('hqk,khd->qhd', weights, value_heads, preferred_element_type=j...  20.9 us
  transfers between devices with their start and end apart: 4, of which 4 were waited for; matrix products, arithmetic and copies ran while one was open for 11% of the time, Pallas kernels for 0%

commit v1 on v0

--- a/solution.py
+++ b/solution.py
@@ -141,7 +141,23 @@
     )
     shift, scale, gate = select_modulation(modulation, own_item, own_text, model_width)
     modded = modulate(tokens, shift, scale)
-    pieces = lax.all_gather(modded, "tensor", axis=0, tiled=True)
+    ways, here, turn = (lax.axis_size("tensor"), lax.axis_index("tensor"), modded.shape[0])
+    dims = [n * ways if d == 0 else n for d, n in enumerate(modded.shape)]
+    full = lax.dynamic_update_slice_in_dim(
+        jnp.zeros(dims, modded.dtype), modded, here * turn, axis=0
+    )
+    going_up = going_down = modded
+    for far in range(1, ways // 2 + 1):
+        going_up = lax.ppermute(going_up, "tensor", [(d, (d + 1) % ways) for d in range(ways)])
+        full = lax.dynamic_update_slice_in_dim(full, going_up, (here - far) % ways * turn, axis=0)
+        if 2 * far < ways:
+            going_down = lax.ppermute(
+                going_down, "tensor", [(d, (d - 1) % ways) for d in range(ways)]
+            )
+            full = lax.dynamic_update_slice_in_dim(
+                full, going_down, (here + far) % ways * turn, axis=0
+            )
+    pieces = full
     projected = jnp.concatenate(
         [
             jnp.dot(pieces, w_query, preferred_element_type=jnp.float32),

time: 768 us -> 799 us (1.040)
  matrix products: 104 us -> 123 us
  local copies, waits for them, and re-layouts: 60.7 us -> 70.7 us
  starting transfers between devices: 0.42 us -> 9.25 us
    all_gather x1 -> x0, waiting for transfers between devices: 24.6 us -> none  [local(): pieces = lax.all_gather(modded, 'tensor', axis=0, tiled=True)]
    ppermute x0 -> x7, waiting for transfers between devices: none -> 24.3 us  [the longest x4 24.3 us: local(): lax.ppermute(going_up, 'tensor', [(d, (d + 1) % ways) for d in range(ways)])]
    dot_general x20, matrix products: 61 us -> 81.5 us  [block_terms(): jnp.einsum('qhd,khd->hqk', query_heads, key_heads, preferred_element_type...]
    ppermute x0 -> x7, starting transfers between devices: none -> 8.87 us  [the longest x3 8.53 us: local(): lax.ppermute(going_down, 'tensor', [(d, (d - 1) % ways) for d in range(wa...]
  transfers between devices with their start and end apart: 4 -> 10, of which waited for: 4 -> 7; matrix products, arithmetic and copies ran while one was open for 11% -> 11% of each run, Pallas kernels for 0% -> 0%
where the time goes in v1:
time: 799 us; the launch traced here: 793 us
  waiting for transfers between devices  365 us (46%)
  blocking collectives  180 us (23%)
  matrix products  123 us (15%)
  local copies, waits for them, and re-layouts  70.7 us (9%)
  other arithmetic  30.6 us (4%)
  between operations  15 us (2%)
  starting transfers between devices  9.25 us (1%)
    all_gather x1, blocking collectives, local(): lax.all_gather(partial_mod, ('row', 'col', 'tensor'), axis=1, tiled=True)  180 us
    all_gather x1, waiting for transfers between devices, local(): value_block = lax.all_gather(value_rows, ('row', 'col'), axis=0, tiled=True)  155 us
    all_gather x1, waiting for transfers between devices, local(): key_block = lax.all_gather(key_rows, ('row', 'col'), axis=0, tiled=True)  152 us
    dot_general x20, matrix products, block_terms(): jnp.einsum('qhd,khd->hqk', query_heads, key_heads, preferred_element_type...  81.5 us
    slice x23, local copies, waits for them, and re-layouts, local(): value_part = value_block[offset:stop]  40.4 us
    reduce_scatter x1, waiting for transfers between devices, local(): lax.psum_scatter(jnp.dot(attended, w_out, preferred_element_type=jnp.floa...  33.5 us
    ppermute x4, waiting for transfers between devices, local(): lax.ppermute(going_up, 'tensor', [(d, (d + 1) % ways) for d in range(ways)])  24.3 us
    dot_general x20, matrix products, block_terms(): jnp.einsum('hqk,khd->qhd', weights, value_heads, preferred_element_type=j...  20.8 us
  transfers between devices with their start and end apart: 10, of which 7 were waited for; matrix products, arithmetic and copies ran while one was open for 11% of the time, Pallas kernels for 0%

profile of v1, /device:TPU:0, one launch (start us, length us, event | category | flops | bytes accessed | tf_op | source)
XLA Modules:
  0.0 793.3 jit_solution(7071441534848822220)
XLA Ops:
  12.6 179.5 %all-gather = f32[128,144,2]{1,2,0:T(2,128)S(1)} all-gather(f32[1,144,2]{1,2,0:T(2,128)S(1)} %convolution_bitcast_fusion.1), channel_id=1, replica_groups=mesh['row'=8,'col'=2,'tensor'=8] {'row','col','tensor'}, dimensions={0}, use_global_device_ids=true | all-gather | bytes 148608 | tf_op jit(solution)/shard_map/all_gather | solution.py:130
  199.8 6.7 collective-permute-done
  211.1 4.9 collective-permute-done.2
  220.6 4.9 collective-permute-done.4
  227.0 7.8 collective-permute-done.6
  235.7 5.1 convolution_convert_fusion.1
  243.3 4.9 fusion.48
  249.8 5.9 fusion.49
  271.5 9.0 %compare_convert_fusion.3 = (f32[640,512]{0,1:T(8,128)}, f32[640,512]{0,1:T(8,128)}, f32[640,512]{0,1:T(8,128)}, f32[640,512]{0,1:T(8,128)}, f32[640,512]{0,1:T(...) fusion(s32[640]{0:T(1024)S(1)} %get-tuple-element.107, ...), kind=kLoop, calls=%fused_computation.62 | loop fusion | flops 11796480 | bytes 23632384 | tf_op jit(solution)/shard_map/convert_element_type | solution.py:193
  282.5 154.9 %all-gather.4.cloned.1.call-done = bf16[10240,384]{1,0:T(8,128)(2,1)} async-done(((bf16[640,384]{1,0:T(8,128)(2,1)}), bf16[10240,384]{1,0:T(8,128)(2,1)}) %all-gather.4.cloned.1.call-update) | async-done | bytes 7864336 | tf_op jit(solution)/shard_map/all_gather | solution.py:182
  437.4 6.1 fusion.45
  477.9 152.2 %all-gather.6.cloned.1.call-done = bf16[10240,384]{0,1:T(8,128)(2,1)} async-done(((bf16[640,384]{0,1:T(8,128)(2,1)}), bf16[10240,384]{0,1:T(8,128)(2,1)}) %all-gather.6.cloned.1.call-update) | async-done | bytes 7864336 | tf_op jit(solution)/shard_map/all_gather | solution.py:181
  630.1 5.5 fusion.44
  662.1 5.7 convert_reduce_fusion.11
  667.8 5.7 convert_reduce_fusion.10
  673.5 5.7 convert_reduce_fusion.9
  679.2 5.7 convert_reduce_fusion.8
  684.9 5.7 convert_reduce_fusion.7
  690.6 5.7 convert_reduce_fusion.6
  696.3 6.2 convert_reduce_fusion.5
  702.5 5.8 convert_reduce_fusion.4
  708.3 5.7 convert_reduce_fusion.2
  716.9 6.0 convert_reduce_fusion.1
  751.0 33.5 %reduce-scatter.2.cloned.1.call-done = bf16[80,3072]{1,0:T(8,128)(2,1)} async-done(((bf16[640,3072]{1,0:T(8,128)(2,1)}), bf16[80,3072]{1,0:T(8,128)(2,1)}) %reduce-scatter.2.cloned.1.call-update) | async-done | bytes 491536 | tf_op jit(solution)/shard_map/reduce_scatter | solution.py:201
  (285 shorter events, 139.8 us)
Async XLA Ops:
  6.5 740.3 %copy-start = (bf16[384,3072]{1,0:T(8,128)(2,1)S(1)}, bf16[384,3072]{1,0:T(8,128)(2,1)}, u32[]{:S(2)}) copy-start(bf16[384,3072]{1,0:T(8,128)(2,1)} %param.15) | copy-start | bytes 7077892
  6.5 187.1 %copy-start.1 = (bf16[80,3072]{1,0:T(8,128)(2,1)S(1)}, bf16[80,3072]{1,0:T(8,128)(2,1)}, u32[]{:S(2)}) copy-start(bf16[80,3072]{1,0:T(8,128)(2,1)} %param.11) | copy-start | bytes 1474564
  6.5 430.9 %all-gather.4.cloned.1.call-start = ((), (), s32[]{:S(2)}) async-start(), calls=%async_computation.1 | async-start | bytes 8355840 | tf_op jit(solution)/shard_map/all_gather | solution.py:182
  11.4 183.5 %copy-start.70 = (pred[80]{0:T(512)(128)(4,1)}, pred[80]{0:T(512)(128)(4,1)S(1)}, u32[]{:S(2)}) copy-start(pred[80]{0:T(512)(128)(4,1)S(1)} %fusion.38) | copy-start | bytes 244
  196.8 9.7 %collective-permute-start = (bf16[80,3072]{1,0:T(8,128)(2,1)}, bf16[80,3072]{1,0:T(8,128)(2,1)S(1)}, u32[]{:S(2)}, u32[]{:S(2)}) collective-permute-start(bf16[80,3072]{1,0:T(8,128)(2,1)} %get-tuple-element.6), channel_id=1, source_target_pairs={{0,1},{1,2},{2,3},{3,4},{4,5},{5,6},{6,7},{7,0},{8,9},{9,10},{10,1... | collective-permute-start | bytes 1474568 | tf_op jit(solution)/shard_map/ppermute | solution.py:151
  197.2 9.3 %collective-permute-start.1 = (bf16[80,3072]{1,0:T(8,128)(2,1)}, bf16[80,3072]{1,0:T(8,128)(2,1)S(1)}, u32[]{:S(2)}, u32[]{:S(2)}) collective-permute-start(bf16[80,3072]{1,0:T(8,128)(2,1)} %get-tuple-element.6), channel_id=1, source_target_pairs={{0,7},{1,0},{2,1},{3,2},{4,3},{5,4},{6,5},{7,6},{8,15},{9,8},{10,9... | collective-permute-start | bytes 1474568 | tf_op jit(solution)/shard_map/ppermute | solution.py:154
  199.8 36.0 %copy-start.76 = (bf16[3072,384]{1,0:T(8,128)(2,1)S(1)}, bf16[3072,384]{1,0:T(8,128)(2,1)}, u32[]{:S(2)}) copy-start(bf16[3072,384]{1,0:T(8,128)(2,1)} %param.14) | copy-start | bytes 7077892
  206.5 9.5 %collective-permute-start.2 = (bf16[80,3072]{1,0:T(8,128)(2,1)S(1)}, bf16[80,3072]{1,0:T(8,128)(2,1)S(1)}, u32[]{:S(2)}, u32[]{:S(2)}) collective-permute-start(bf16[80,3072]{1,0:T(8,128)(2,1)S(1)} %collective-permute-done), channel_id=1, source_target_pairs={{0,1},{1,2},{2,3},{3,4},{4,5},{5,6},{6,7},{7,0},{8,9},{9,10},{10,1... | collective-permute-start | bytes 1474568 | tf_op jit(solution)/shard_map/ppermute | solution.py:151
  206.5 9.5 %collective-permute-start.3 = (bf16[80,3072]{1,0:T(8,128)(2,1)S(1)}, bf16[80,3072]{1,0:T(8,128)(2,1)S(1)}, u32[]{:S(2)}, u32[]{:S(2)}) collective-permute-start(bf16[80,3072]{1,0:T(8,128)(2,1)S(1)} %collective-permute-done.1), channel_id=1, source_target_pairs={{0,7},{1,0},{2,1},{3,2},{4,3},{5,4},{6,5},{7,6},{8,15},{9,8},{10,9... | collective-permute-start | bytes 1474568 | tf_op jit(solution)/shard_map/ppermute | solution.py:154
  216.0 9.5 %collective-permute-start.4 = (bf16[80,3072]{1,0:T(8,128)(2,1)S(1)}, bf16[80,3072]{1,0:T(8,128)(2,1)S(1)}, u32[]{:S(2)}, u32[]{:S(2)}) collective-permute-start(bf16[80,3072]{1,0:T(8,128)(2,1)S(1)} %collective-permute-done.2), channel_id=1, source_target_pairs={{0,1},{1,2},{2,3},{3,4},{4,5},{5,6},{6,7},{7,0},{8,9},{9,10},{10,1... | collective-permute-start | bytes 1474568 | tf_op jit(solution)/shard_map/ppermute | solution.py:151
  216.0 10.3 %collective-permute-start.5 = (bf16[80,3072]{1,0:T(8,128)(2,1)S(1)}, bf16[80,3072]{1,0:T(8,128)(2,1)S(1)}, u32[]{:S(2)}, u32[]{:S(2)}) collective-permute-start(bf16[80,3072]{1,0:T(8,128)(2,1)S(1)} %collective-permute-done.3), channel_id=1, source_target_pairs={{0,7},{1,0},{2,1},{3,2},{4,3},{5,4},{6,5},{7,6},{8,15},{9,8},{10,9... | collective-permute-start | bytes 1474568 | tf_op jit(solution)/shard_map/ppermute | solution.py:154
  225.4 9.5 %collective-permute-start.6 = (bf16[80,3072]{1,0:T(8,128)(2,1)S(1)}, bf16[80,3072]{1,0:T(8,128)(2,1)S(1)}, u32[]{:S(2)}, u32[]{:S(2)}) collective-permute-start(bf16[80,3072]{1,0:T(8,128)(2,1)S(1)} %collective-permute-done.4), channel_id=1, source_target_pairs={{0,1},{1,2},{2,3},{3,4},{4,5},{5,6},{6,7},{7,0},{8,9},{9,10},{10,1... | collective-permute-start | bytes 1474568 | tf_op jit(solution)/shard_map/ppermute | solution.py:151
  235.7 6.2 copy-start.75
  235.7 7.0 copy-start.72
  240.9 389.2 %all-gather.6.cloned.1.call-start = ((), (), s32[]{:S(2)}) async-start(), calls=%async_computation.2 | async-start | bytes 8355840 | tf_op jit(solution)/shard_map/all_gather | solution.py:181
  269.4 515.1 %reduce-scatter.2.cloned.1.call-start = ((), (), s32[]{:S(2)}) async-start(), calls=%async_computation.3 | async-start | bytes 4423680 | tf_op jit(solution)/shard_map/reduce_scatter | solution.py:201
  271.5 9.0 %copy-start.11 = (bf16[640,6,32,1]{0,3,2,1:T(2,128)(2,1)S(1)}, bf16[640,6,32,1]{0,3,2,1:T(2,128)(2,1)}, u32[]{:S(2)}) copy-start(bf16[640,6,32,1]{0,3,2,1:T(2,128)(2,1)} %get-tuple-element.52) | copy-start | bytes 737284
  437.4 7.3 slice-start
  696.3 6.2 copy-start.41
  751.0 33.5 %copy-start.51 = (f32[1,3072]{1,0:T(1,128)S(1)}, f32[1,3072]{1,0:T(1,128)}, u32[]{:S(2)}) copy-start(f32[1,3072]{1,0:T(1,128)} %get-tuple-element.53) | copy-start | bytes 36868
  751.0 33.5 %copy-start.52 = (f32[1,3072]{1,0:T(1,128)S(1)}, f32[1,3072]{1,0:T(1,128)}, u32[]{:S(2)}) copy-start(f32[1,3072]{1,0:T(1,128)} %get-tuple-element.62) | copy-start | bytes 36868
  751.0 33.5 %copy-start.53 = (f32[1,3072]{1,0:T(1,128)S(1)}, f32[1,3072]{1,0:T(1,128)}, u32[]{:S(2)}) copy-start(f32[1,3072]{1,0:T(1,128)} %get-tuple-element.63) | copy-start | bytes 36868
  751.0 33.5 %copy-start.54 = (f32[1,3072]{1,0:T(1,128)S(1)}, f32[1,3072]{1,0:T(1,128)}, u32[]{:S(2)}) copy-start(f32[1,3072]{1,0:T(1,128)} %get-tuple-element.64) | copy-start | bytes 36868
  751.0 33.5 %copy-start.71 = (pred[80]{0:T(512)(128)(4,1)S(1)}, pred[80]{0:T(512)(128)(4,1)}, u32[]{:S(2)}) copy-start(pred[80]{0:T(512)(128)(4,1)} %copy-done.70) | copy-start | bytes 244
  (65 other events, 165.2 us)
Sparse Core Ops, SparseCore 0:
  241.0 196.3 all-gather.3
  439.1 190.9 all-gather.5
  751.2 33.2 reduce-scatter.1
